TPU v7x, 32 devices: a whole 2x2x4 slice. The times are simulated.
32 devices in a mesh: gx: 4 (over z), gy: 2 (over x), gz: 4 (over y, core).
Axes of the slice: x: 2, y: 2, z: 4, core: 2. Of those that a mesh axis runs over, the one named last changes fastest.
Arguments:
- queries: bfloat16 [64, 1024, 512], P(('gx', 'gy'), 'gz'), may hold values from -48 to 48
- key_vectors: bfloat16 [64, 1024, 128], P(('gx', 'gy'), 'gz'), may hold values from -12 to 12
- value_vectors: bfloat16 [64, 1024, 128], P(('gx', 'gy'), 'gz'), may hold values from -6 to 6
- chosen: int32 [64, 2], P(('gx', 'gy')), may hold values from -1 to 63, as said below
Outputs:
- attended: bfloat16 [64, 1024, 512], P(('gx', 'gy'), 'gz')
Inputs may be any that keep to these rules, and one draw needn't show every extreme that they name: `chosen`: both entries of a row are -1, or both are blocks of two different groups before the row's own group, counting blocks in groups of 8 consecutive blocks. One group's rows name blocks of any one group in at most 1 entries; every group from the third on names blocks of the first group in exactly 1 entries. The rows of the first two groups are all -1.
All inputs are finite; a program needn't handle non-finite values.
Results may differ from a plain program's by a relative error of at most 0.0042.
Values may be sent and summed in bfloat16 or wider, within the bound.
No kernel may reach another device: no remote copies, remote signals or barrier semaphores. Data moves between devices by JAX's collectives and lax.ppermute only.
A program may use at most 128 MiB of HBM per device.

v0:
```python
import jax
import jax.numpy as jnp
from jax import lax
from jax.sharding import PartitionSpec as P

CAP = 1


def allowed_mask(token_start, query_count, head_count, block_len, live_pair):
    token_pos = token_start + jnp.arange(query_count * head_count, dtype=jnp.int32) // head_count
    key_pos = jnp.arange(3 * block_len, dtype=jnp.int32)
    own_part = (key_pos[None, :] < block_len) & (key_pos[None, :] <= token_pos[:, None])
    pair_slot = jnp.clip(key_pos // block_len - 1, 0, 1)
    far_part = (key_pos >= block_len) & (live_pair[pair_slot] > 0)
    return own_part | far_part[None, :]


def attend_block(query_block, key_sets, value_sets, allowed):
    head_dim = key_sets.shape[1]
    flat_queries = query_block.reshape(-1, head_dim)
    scores = jnp.dot(flat_queries, key_sets.T, preferred_element_type=jnp.float32) * head_dim ** (
        -0.5
    )
    scores = jnp.where(allowed, scores, -jnp.inf)
    row_top = jnp.max(scores, axis=1, keepdims=True)
    weights = jnp.exp(scores - row_top)
    row_total = jnp.sum(weights, axis=1, keepdims=True)
    mixed = (
        jnp.dot(weights.astype(jnp.bfloat16), value_sets, preferred_element_type=jnp.float32)
        / row_total
    )
    return mixed.astype(jnp.bfloat16).reshape(query_block.shape)


def body(queries, key_vectors, value_vectors, chosen):
    blocks_here, quarter, row_width = queries.shape
    head_dim = key_vectors.shape[2]
    head_count = row_width // head_dim
    groups = lax.axis_size(("gx", "gy"))
    quarter_index = lax.axis_index("gz")
    entries = chosen.reshape(-1)
    entry_count = entries.shape[0]
    live_entry = entries >= 0
    owner_group = jnp.where(live_entry, entries // blocks_here, -1)
    local_block = jnp.where(live_entry, entries % blocks_here, 0)
    entry_ids = jnp.arange(entry_count, dtype=jnp.int32)
    same_owner = (owner_group[:, None] == owner_group[None, :]) & live_entry[None, :]
    slot_rank = jnp.sum(same_owner & (entry_ids[None, :] < entry_ids[:, None]), axis=1)
    group_ids = jnp.arange(groups, dtype=jnp.int32)
    slot_ids = jnp.arange(CAP, dtype=jnp.int32)
    hits = (owner_group[:, None, None] == group_ids[None, :, None]) & (
        slot_rank[:, None, None] == slot_ids[None, None, :]
    )
    want_table = jnp.sum(jnp.where(hits, local_block[:, None, None] + 1, 0), axis=0)
    requests = lax.all_to_all(want_table, ("gx", "gy"), split_axis=0, concat_axis=0, tiled=True)
    paired = jnp.concatenate([key_vectors, value_vectors], axis=2)
    wanted = jnp.maximum(requests - 1, 0).reshape(-1)
    outgoing = jnp.take(paired, wanted, axis=0).reshape(groups, CAP, quarter, 2 * head_dim)
    incoming = lax.all_to_all(outgoing, ("gx", "gy"), split_axis=0, concat_axis=0, tiled=True)
    incoming = incoming.reshape(groups * CAP, quarter, 2 * head_dim)
    flat_slot = jnp.maximum(owner_group, 0) * CAP + jnp.minimum(slot_rank, CAP - 1)
    fetched = jnp.take(incoming, flat_slot, axis=0)
    fetched_full, own_blocks = (
        lax.all_gather(fetched, "gz", axis=1, tiled=True),
        lax.all_gather(paired, "gz", axis=1, tiled=True),
    )
    block_len = fetched_full.shape[1]
    pair_blocks = fetched_full.reshape(blocks_here, 2, block_len, 2 * head_dim)
    live_pairs = live_entry.astype(jnp.int32).reshape(blocks_here, 2)

    def one_block(operands):
        query_block, own_pair, far_pair, live_pair = operands
        key_sets = jnp.concatenate(
            [own_pair[:, :head_dim], far_pair[0, :, :head_dim], far_pair[1, :, :head_dim]], axis=0
        )
        value_sets = jnp.concatenate(
            [own_pair[:, head_dim:], far_pair[0, :, head_dim:], far_pair[1, :, head_dim:]], axis=0
        )
        allowed = allowed_mask(quarter_index * quarter, quarter, head_count, block_len, live_pair)
        return attend_block(query_block, key_sets, value_sets, allowed)

    return lax.map(one_block, (queries, own_blocks, pair_blocks, live_pairs))


def solution(mesh):
    placed = (
        P(("gx", "gy"), "gz", None),
        P(("gx", "gy"), "gz", None),
        P(("gx", "gy"), "gz", None),
        P(("gx", "gy"), None),
    )
    return jax.shard_map(
        body, mesh=mesh, in_specs=placed, out_specs=P(("gx", "gy"), "gz", None), check_vma=False
    )
```

profile of v0, /device:TPU:0, one launch (start us, length us, event | category | flops | bytes accessed | tf_op | source)
XLA Modules:
  0.0 239.3 jit_solution(9529049361917233739)
XLA Ops:
  10.5 13.6 %all_to_all.14 = s32[8,1,1]{2,1,0:T(1,128)S(1)} all-to-all(s32[8,1,1]{2,1,0:T(1,128)S(1)} %copy.16), channel_id=1, replica_groups=mesh['gx'=4,'gy'=2,'gz'=4] {'gx','gy'}, dimensions={0} | all-to-all | bytes 64 | tf_op jit(solution)/shard_map/all_to_all | solution.py:55
  24.3 1.8 gather_fusion
  27.5 3.6 %all-to-all-start.1 = ((bf16[8,1,256,256]{3,2,1,0:T(8,128)(2,1)}), bf16[8,1,256,256]{3,2,1,0:T(8,128)(2,1)S(1)}, u32[]{:S(2)}, u32[]{:S(2)}) async-start(bf16[8,1,256,256]{3,2,1,0:T(8,128)(2,1)} %bitcast_select_fusion), calls=%async_computation.1 | async-start | bytes 2097152 | tf_op jit(solution)/shard_map/all_to_all | solution.py:59
  31.2 24.6 %all-to-all-done.1 = bf16[8,1,256,256]{3,2,1,0:T(8,128)(2,1)S(1)} async-done(((bf16[8,1,256,256]{3,2,1,0:T(8,128)(2,1)}), bf16[8,1,256,256]{3,2,1,0:T(8,128)(2,1)S(1)}, u32[]{:S(2)}, u32[]{:S(2)}) %all-to-all-start.1) | async-done | bytes 1048608 | tf_op jit(solution)/shard_map/all_to_all | solution.py:59
  56.5 1.6 broadcast_select_fusion
  58.2 57.3 %all-gather.5.cloned.1.call-done = bf16[16,1024,256]{2,1,0:T(8,128)(2,1)} async-done(((bf16[16,256,256]{2,1,0:T(8,128)(2,1)}), bf16[16,1024,256]{2,1,0:T(8,128)(2,1)}) %all-gather.5.cloned.1.call-update) | async-done | bytes 8388624 | tf_op jit(solution)/shard_map/all_gather | solution.py:64
  115.5 117.0 %while.13 = (s32[]{:T(128)}, bf16[8,256,512]{2,1,0:T(8,128)(2,1)}, s32[]{:T(128)}, s32[8,2]{0,1:T(2,128)S(1)}, bf16[8,256,512]{2,1,0:T(8,128)(2,1)}, /*index=5*/...) while((s32[]{:T(128)}, bf16[8,256,512]{2,1,0:T(8,128)(2,1)}, s32[]{:T(128)}, ...), condition=%wide.region_5.6_spmd, body=%wide.region_2.5_spmd.sunk | while | flops 1647116288 | bytes 48282256 | solution.py:82
  116.1 1.3 compare_reduce_fusion.3
  121.2 4.1 %fusion.58 = (f32[1024]{0:T(1024)S(1)}, f32[1024,3072]{1,0:T(8,128)S(1)}) fusion(bf16[1024,128]{1,0:T(8,128)(2,1)S(1)} %reshape.508, bf16[1024,128]{1,0:T(8,128)(2,1)S(1)} %get-tuple-element.211, bf16[1024,128]{1,0:T(8,128)(2,1)S(1)} %get-tuple-element.212, bf16[1024,128]{1,0:T(8,128)(2,1)S(1)} %get-tuple-element.213, ...), kind=kOutput, calls=%fused_computation.92.clone.1 | convolution fusion | flops 826539008 | bytes 13645824 | tf_op jit(solution)/shard_map/while/body/eval_jaxpr/dot_general | solution.py:21
  125.3 1.9 fusion.59
  127.2 2.0 fusion.60
  135.9 4.1 %fusion.58 = (f32[1024]{0:T(1024)S(1)}, f32[1024,3072]{1,0:T(8,128)S(1)}) fusion(bf16[1024,128]{1,0:T(8,128)(2,1)S(1)} %reshape.508, bf16[1024,128]{1,0:T(8,128)(2,1)S(1)} %get-tuple-element.211, bf16[1024,128]{1,0:T(8,128)(2,1)S(1)} %get-tuple-element.212, bf16[1024,128]{1,0:T(8,128)(2,1)S(1)} %get-tuple-element.213, ...), kind=kOutput, calls=%fused_computation.92.clone.1 | convolution fusion | flops 826539008 | bytes 13645824 | tf_op jit(solution)/shard_map/while/body/eval_jaxpr/dot_general | solution.py:21
  140.0 1.9 fusion.59
  141.8 2.0 fusion.60
  150.5 4.1 %fusion.58 = (f32[1024]{0:T(1024)S(1)}, f32[1024,3072]{1,0:T(8,128)S(1)}) fusion(bf16[1024,128]{1,0:T(8,128)(2,1)S(1)} %reshape.508, bf16[1024,128]{1,0:T(8,128)(2,1)S(1)} %get-tuple-element.211, bf16[1024,128]{1,0:T(8,128)(2,1)S(1)} %get-tuple-element.212, bf16[1024,128]{1,0:T(8,128)(2,1)S(1)} %get-tuple-element.213, ...), kind=kOutput, calls=%fused_computation.92.clone.1 | convolution fusion | flops 826539008 | bytes 13645824 | tf_op jit(solution)/shard_map/while/body/eval_jaxpr/dot_general | solution.py:21
  154.6 1.9 fusion.59
  156.4 2.0 fusion.60
  165.1 4.1 %fusion.58 = (f32[1024]{0:T(1024)S(1)}, f32[1024,3072]{1,0:T(8,128)S(1)}) fusion(bf16[1024,128]{1,0:T(8,128)(2,1)S(1)} %reshape.508, bf16[1024,128]{1,0:T(8,128)(2,1)S(1)} %get-tuple-element.211, bf16[1024,128]{1,0:T(8,128)(2,1)S(1)} %get-tuple-element.212, bf16[1024,128]{1,0:T(8,128)(2,1)S(1)} %get-tuple-element.213, ...), kind=kOutput, calls=%fused_computation.92.clone.1 | convolution fusion | flops 826539008 | bytes 13645824 | tf_op jit(solution)/shard_map/while/body/eval_jaxpr/dot_general | solution.py:21
  169.2 1.9 fusion.59
  171.1 2.0 fusion.60
  179.7 4.1 %fusion.58 = (f32[1024]{0:T(1024)S(1)}, f32[1024,3072]{1,0:T(8,128)S(1)}) fusion(bf16[1024,128]{1,0:T(8,128)(2,1)S(1)} %reshape.508, bf16[1024,128]{1,0:T(8,128)(2,1)S(1)} %get-tuple-element.211, bf16[1024,128]{1,0:T(8,128)(2,1)S(1)} %get-tuple-element.212, bf16[1024,128]{1,0:T(8,128)(2,1)S(1)} %get-tuple-element.213, ...), kind=kOutput, calls=%fused_computation.92.clone.1 | convolution fusion | flops 826539008 | bytes 13645824 | tf_op jit(solution)/shard_map/while/body/eval_jaxpr/dot_general | solution.py:21
  183.8 1.9 fusion.59
  185.7 2.0 fusion.60
  194.3 4.1 %fusion.58 = (f32[1024]{0:T(1024)S(1)}, f32[1024,3072]{1,0:T(8,128)S(1)}) fusion(bf16[1024,128]{1,0:T(8,128)(2,1)S(1)} %reshape.508, bf16[1024,128]{1,0:T(8,128)(2,1)S(1)} %get-tuple-element.211, bf16[1024,128]{1,0:T(8,128)(2,1)S(1)} %get-tuple-element.212, bf16[1024,128]{1,0:T(8,128)(2,1)S(1)} %get-tuple-element.213, ...), kind=kOutput, calls=%fused_computation.92.clone.1 | convolution fusion | flops 826539008 | bytes 13645824 | tf_op jit(solution)/shard_map/while/body/eval_jaxpr/dot_general | solution.py:21
  198.4 1.9 fusion.59
  200.3 2.0 fusion.60
  209.0 4.1 %fusion.58 = (f32[1024]{0:T(1024)S(1)}, f32[1024,3072]{1,0:T(8,128)S(1)}) fusion(bf16[1024,128]{1,0:T(8,128)(2,1)S(1)} %reshape.508, bf16[1024,128]{1,0:T(8,128)(2,1)S(1)} %get-tuple-element.211, bf16[1024,128]{1,0:T(8,128)(2,1)S(1)} %get-tuple-element.212, bf16[1024,128]{1,0:T(8,128)(2,1)S(1)} %get-tuple-element.213, ...), kind=kOutput, calls=%fused_computation.92.clone.1 | convolution fusion | flops 826539008 | bytes 13645824 | tf_op jit(solution)/shard_map/while/body/eval_jaxpr/dot_general | solution.py:21
  213.0 1.9 fusion.59
  214.9 2.0 fusion.60
  223.6 4.1 %fusion.58 = (f32[1024]{0:T(1024)S(1)}, f32[1024,3072]{1,0:T(8,128)S(1)}) fusion(bf16[1024,128]{1,0:T(8,128)(2,1)S(1)} %reshape.508, bf16[1024,128]{1,0:T(8,128)(2,1)S(1)} %get-tuple-element.211, bf16[1024,128]{1,0:T(8,128)(2,1)S(1)} %get-tuple-element.212, bf16[1024,128]{1,0:T(8,128)(2,1)S(1)} %get-tuple-element.213, ...), kind=kOutput, calls=%fused_computation.92.clone.1 | convolution fusion | flops 826539008 | bytes 13645824 | tf_op jit(solution)/shard_map/while/body/eval_jaxpr/dot_general | solution.py:21
  227.7 1.9 fusion.59
  229.5 2.0 fusion.60
  (132 shorter events, 57.9 us)
Async XLA Ops:
  6.5 3.3 %copy-start.1 = (s32[8,2]{0,1:T(2,128)S(1)}, s32[8,2]{0,1:T(2,128)}, u32[]{:S(2)}) copy-start(s32[8,2]{0,1:T(2,128)} %param.9) | copy-start | bytes 196
  6.5 51.7 %all-gather.3.cloned.1.call-start = ((), (), s32[]{:S(2)}) async-start(), calls=%async_computation.2 | async-start | bytes 5242880 | tf_op jit(solution)/shard_map/all_gather | solution.py:65
  8.9 1.0 copy-start
  27.5 28.3 %all-to-all-start.1 = ((bf16[8,1,256,256]{3,2,1,0:T(8,128)(2,1)}), bf16[8,1,256,256]{3,2,1,0:T(8,128)(2,1)S(1)}, u32[]{:S(2)}, u32[]{:S(2)}) async-start(bf16[8,1,256,256]{3,2,1,0:T(8,128)(2,1)} %bitcast_select_fusion), calls=%async_computation.1 | async-start | bytes 2097152 | tf_op jit(solution)/shard_map/all_to_all | solution.py:59
  31.1 84.4 %all-gather.5.cloned.1.call-start = ((), (), s32[]{:S(2)}) async-start(), calls=%async_computation.3 | async-start | bytes 10485760 | tf_op jit(solution)/shard_map/all_gather | solution.py:64
Sparse Core Ops, SparseCore 0:
  10.0 37.1 all-gather.2
  58.3 57.1 all-gather.4
where the time goes:
time: 241 us; the launch traced here: 239 us
  waiting for transfers between devices  81.9 us (34%)
  matrix products  48.7 us (20%)
  local copies, waits for them, and re-layouts  48.4 us (20%)
  other arithmetic  29.1 us (12%)
  blocking collectives  13.6 us (6%)
  between operations  13.5 us (6%)
  starting transfers between devices  3.61 us (1%)
    all_gather x1, waiting for transfers between devices, body(): lax.all_gather(fetched, 'gz', axis=1, tiled=True)  57.3 us
    dot_general x8, matrix products, attend_block(): jnp.dot(flat_queries, key_sets.T, preferred_element_type=jnp.float32)  32.7 us
    all_to_all x1, waiting for transfers between devices, body(): lax.all_to_all(outgoing, ('gx', 'gy'), split_axis=0, concat_axis=0, tiled...  24.6 us
    squeeze x16, local copies, waits for them, and re-layouts, body(): return lax.map(one_block, (queries, own_blocks, pair_blocks, live_pairs))  19.1 us
    dot_general x8, matrix products, attend_block(): jnp.dot(weights.astype(jnp.bfloat16), value_sets, preferred_element_type=...  16.1 us
    reduce_sum x8, other arithmetic, attend_block(): row_total = jnp.sum(weights, axis=1, keepdims=True)  14.9 us
    all_to_all x1, blocking collectives, body(): lax.all_to_all(want_table, ('gx', 'gy'), split_axis=0, concat_axis=0, til...  13.6 us
    gt x8, other arithmetic, allowed_mask(): far_part = (key_pos >= block_len) & (live_pair[pair_slot] > 0)  10.5 us
  transfers between devices with their start and end apart: 3, of which 2 were waited for; matrix products, arithmetic and copies ran while one was open for 3% of the time, Pallas kernels for 0%

commit v1 on v0

--- a/solution.py
+++ b/solution.py
@@ -4,6 +4,22 @@
 from jax.sharding import PartitionSpec as P
 
 CAP = 1
+
+
+def _follow_chunk(local_values, dimension_no, inner_x):
+    state_now, later = (local_values.shape[:dimension_no], local_values.shape[dimension_no + 1 :])
+    value_now = local_values.reshape(*state_now, inner_x, -1, *later)
+    f_now = jnp.moveaxis(value_now, dimension_no, 0)
+    return f_now
+
+
+def obtain_edge_up(local_x, row_dim):
+    local_x = jnp.moveaxis(local_x, 0, row_dim)
+    all_rows = local_x.shape
+    earlier = local_x.reshape(
+        *all_rows[:row_dim], all_rows[row_dim] * all_rows[row_dim + 1], *all_rows[row_dim + 2 :]
+    )
+    return earlier
 
 
 def allowed_mask(token_start, query_count, head_count, block_len, live_pair):
@@ -52,7 +68,20 @@
         slot_rank[:, None, None] == slot_ids[None, None, :]
     )
     want_table = jnp.sum(jnp.where(hits, local_block[:, None, None] + 1, 0), axis=0)
-    requests = lax.all_to_all(want_table, ("gx", "gy"), split_axis=0, concat_axis=0, tiled=True)
+    local_now = jax.lax.axis_size(("gx", "gy"))
+    state_next = jax.lax.axis_index(("gx", "gy"))
+    y_new, low = (local_now, state_next)
+    a_next = _follow_chunk(want_table, 0, y_new)
+    history = [a_next[low]]
+    for src_i in range(1, y_new):
+        z1 = a_next[low ^ src_i]
+        lower = jax.lax.ppermute(
+            z1, axis_name=("gx", "gy"), perm=[(d, d ^ src_i) for d in range(y_new)]
+        )
+        history.append(lower)
+    extra = jnp.stack(history, axis=0)
+    a_next = extra[low ^ jnp.arange(y_new)]
+    requests = obtain_edge_up(a_next, 0)
     paired = jnp.concatenate([key_vectors, value_vectors], axis=2)
     wanted = jnp.maximum(requests - 1, 0).reshape(-1)
     outgoing = jnp.take(paired, wanted, axis=0).reshape(groups, CAP, quarter, 2 * head_dim)

time: 241 us -> 250 us (1.037)
  blocking collectives: 13.6 us -> 0 us
  starting transfers between devices: 3.61 us -> 16.1 us
  local copies, waits for them, and re-layouts: 48.4 us -> 54.6 us
  waiting for transfers between devices: 81.9 us -> 86.8 us
    all_to_all x1 -> x0, blocking collectives: 13.6 us -> none  [body(): lax.all_to_all(want_table, ('gx', 'gy'), split_axis=0, concat_axis=0, til...]
    ppermute x0 -> x7, starting transfers between devices: none -> 12.5 us  [body(): jax.lax.ppermute(z1, axis_name=('gx', 'gy'), perm=[(d, d ^ src_i) for d i...]
    ppermute x0 -> x7, waiting for transfers between devices: none -> 6.45 us  [body(): jax.lax.ppermute(z1, axis_name=('gx', 'gy'), perm=[(d, d ^ src_i) for d i...]
    another operation x0 -> x2, local copies, waits for them, and re-layouts: none -> 5.92 us  [the longest x1 5.21 us: body(): extra = jnp.stack(history, axis=0)]
  transfers between devices with their start and end apart: 3 -> 10, of which waited for: 2 -> 5; matrix products, arithmetic and copies ran while one was open for 3% -> 5% of each run, Pallas kernels for 0% -> 0%
where the time goes in v1:
time: 250 us; the launch traced here: 249 us
  waiting for transfers between devices  86.8 us (35%)
  local copies, waits for them, and re-layouts  54.6 us (22%)
  matrix products  48.9 us (20%)
  other arithmetic  28.3 us (11%)
  starting transfers between devices  16.1 us (6%)
  between operations  13.6 us (5%)
    all_gather x1, waiting for transfers between devices, body(): lax.all_gather(fetched, 'gz', axis=1, tiled=True)  57.2 us
    dot_general x8, matrix products, attend_block(): jnp.dot(flat_queries, key_sets.T, preferred_element_type=jnp.float32)  32.8 us
    all_to_all x1, waiting for transfers between devices, body(): lax.all_to_all(outgoing, ('gx', 'gy'), split_axis=0, concat_axis=0, tiled...  23 us
    squeeze x16, local copies, waits for them, and re-layouts, body(): return lax.map(one_block, (queries, own_blocks, pair_blocks, live_pairs))  19.1 us
    dot_general x8, matrix products, attend_block(): jnp.dot(weights.astype(jnp.bfloat16), value_sets, preferred_element_type=...  16.1 us
    reduce_sum x8, other arithmetic, attend_block(): row_total = jnp.sum(weights, axis=1, keepdims=True)  14.8 us
    ppermute x7, starting transfers between devices, body(): jax.lax.ppermute(z1, axis_name=('gx', 'gy'), perm=[(d, d ^ src_i) for d i...  12.5 us
    gt x8, other arithmetic, allowed_mask(): far_part = (key_pos >= block_len) & (live_pair[pair_slot] > 0)  10.2 us
  transfers between devices with their start and end apart: 10, of which 5 were waited for; matrix products, arithmetic and copies ran while one was open for 5% of the time, Pallas kernels for 0%

profile of v1, /device:TPU:0, one launch (start us, length us, event | category | flops | bytes accessed | tf_op | source)
XLA Modules:
  0.0 248.7 jit_solution(170155633899455180)
XLA Ops:
  11.1 3.0 %collective-permute-start = (s32[1,1]{1,0:T(1,128)}, s32[1,1]{1,0:T(1,128)}, u32[]{:S(2)}, u32[]{:S(2)}) collective-permute-start(s32[1,1]{1,0:T(1,128)} %bitcast.9), channel_id=1, source_target_pairs={{0,4},{4,0},{8,12},{12,8},{16,20},{20,16},{24,28},{28,24},{1,5},{5... | collective-permute-start | bytes 20 | tf_op jit(solution)/shard_map/ppermute | solution.py:78
  15.7 3.0 %collective-permute-start.3 = (s32[1,1]{1,0:T(1,128)}, s32[1,1]{1,0:T(1,128)}, u32[]{:S(2)}, u32[]{:S(2)}) collective-permute-start(s32[1,1]{1,0:T(1,128)} %bitcast.15), channel_id=1, source_target_pairs={{0,16},{4,20},{8,24},{12,28},{16,0},{20,4},{24,8},{28,12},{1,17},{... | collective-permute-start | bytes 20 | tf_op jit(solution)/shard_map/ppermute | solution.py:78
  20.0 3.7 %collective-permute-start.5 = (s32[1,1]{1,0:T(1,128)}, s32[1,1]{1,0:T(1,128)}, u32[]{:S(2)}, u32[]{:S(2)}) collective-permute-start(s32[1,1]{1,0:T(1,128)} %bitcast.19), channel_id=1, source_target_pairs={{0,24},{4,28},{8,16},{12,20},{16,8},{20,12},{24,0},{28,4},{1,25},{... | collective-permute-start | bytes 20 | tf_op jit(solution)/shard_map/ppermute | solution.py:78
  25.6 4.6 %collective-permute-done.6 = s32[1,1]{1,0:T(1,128)} collective-permute-done((s32[1,1]{1,0:T(1,128)}, s32[1,1]{1,0:T(1,128)}, u32[]{:S(2)}, u32[]{:S(2)}) %collective-permute-start.6) | collective-permute-done | bytes 36 | tf_op jit(solution)/shard_map/ppermute | solution.py:78
  30.1 5.2 %stack.31 = s32[8,1,1]{0,2,1:T(1,128)S(1)} concatenate(s32[1,1,1]{0,2,1:T(1,128)} %bitcast.8, s32[1,1,1]{0,2,1:T(1,128)} %bitcast.10, s32[1,1,1]{0,2,1:T(1,128)} %bitcast.12, s32[1,1,1]{0,2,1:T(1,128)} %bitcast.14, s32[1,1,1]{0,2,1:T(1,128)} %bitcast.16, s32[1,1,1]{0,2,1:T(1,128)} %bitcast.18, s32[1,1,1]{0,2,1:T(1,128)} %bitcast.20, s32[1,1,1]{0,2,1:T(1,128)} %bitcast.22), dimensions={0} | concatenate | bytes 64 | tf_op jit(solution)/shard_map/stack | solution.py:82
  39.0 3.6 %all-to-all-start = ((bf16[8,1,256,256]{3,2,1,0:T(8,128)(2,1)}), bf16[8,1,256,256]{3,2,1,0:T(8,128)(2,1)S(1)}, u32[]{:S(2)}, u32[]{:S(2)}) async-start(bf16[8,1,256,256]{3,2,1,0:T(8,128)(2,1)} %bitcast_select_fusion), calls=%async_computation | async-start | bytes 2097152 | tf_op jit(solution)/shard_map/all_to_all | solution.py:88
  42.7 23.0 %all-to-all-done = bf16[8,1,256,256]{3,2,1,0:T(8,128)(2,1)S(1)} async-done(((bf16[8,1,256,256]{3,2,1,0:T(8,128)(2,1)}), bf16[8,1,256,256]{3,2,1,0:T(8,128)(2,1)S(1)}, u32[]{:S(2)}, u32[]{:S(2)}) %all-to-all-start) | async-done | bytes 1048608 | tf_op jit(solution)/shard_map/all_to_all | solution.py:88
  68.1 57.2 %all-gather.5.cloned.1.call-done = bf16[16,1024,256]{2,1,0:T(8,128)(2,1)} async-done(((bf16[16,256,256]{2,1,0:T(8,128)(2,1)}), bf16[16,1024,256]{2,1,0:T(8,128)(2,1)}) %all-gather.5.cloned.1.call-update) | async-done | bytes 8388624 | tf_op jit(solution)/shard_map/all_gather | solution.py:93
  125.3 116.5 %while.13 = (s32[]{:T(128)}, bf16[8,256,512]{2,1,0:T(8,128)(2,1)}, s32[]{:T(128)}, s32[8,2]{0,1:T(2,128)S(1)}, bf16[8,256,512]{2,1,0:T(8,128)(2,1)}, /*index=5*/...) while((s32[]{:T(128)}, bf16[8,256,512]{2,1,0:T(8,128)(2,1)}, s32[]{:T(128)}, ...), condition=%wide.region_5.6_spmd, body=%wide.region_2.5_spmd.sunk | while | flops 1647116288 | bytes 48282256 | solution.py:111
  131.0 4.1 %fusion.59 = (f32[1024]{0:T(1024)S(1)}, f32[1024,3072]{1,0:T(8,128)S(1)}) fusion(bf16[1024,128]{1,0:T(8,128)(2,1)S(1)} %reshape.574, bf16[1024,128]{1,0:T(8,128)(2,1)S(1)} %get-tuple-element.219, bf16[1024,128]{1,0:T(8,128)(2,1)S(1)} %get-tuple-element.220, bf16[1024,128]{1,0:T(8,128)(2,1)S(1)} %get-tuple-element.221, ...), kind=kOutput, calls=%fused_computation.95.clone.1 | convolution fusion | flops 826539008 | bytes 13645824 | tf_op jit(solution)/shard_map/while/body/eval_jaxpr/dot_general | solution.py:37
  137.0 2.0 fusion.61
  145.6 4.1 %fusion.59 = (f32[1024]{0:T(1024)S(1)}, f32[1024,3072]{1,0:T(8,128)S(1)}) fusion(bf16[1024,128]{1,0:T(8,128)(2,1)S(1)} %reshape.574, bf16[1024,128]{1,0:T(8,128)(2,1)S(1)} %get-tuple-element.219, bf16[1024,128]{1,0:T(8,128)(2,1)S(1)} %get-tuple-element.220, bf16[1024,128]{1,0:T(8,128)(2,1)S(1)} %get-tuple-element.221, ...), kind=kOutput, calls=%fused_computation.95.clone.1 | convolution fusion | flops 826539008 | bytes 13645824 | tf_op jit(solution)/shard_map/while/body/eval_jaxpr/dot_general | solution.py:37
  149.7 1.9 fusion.60
  151.5 2.0 fusion.61
  160.2 4.1 %fusion.59 = (f32[1024]{0:T(1024)S(1)}, f32[1024,3072]{1,0:T(8,128)S(1)}) fusion(bf16[1024,128]{1,0:T(8,128)(2,1)S(1)} %reshape.574, bf16[1024,128]{1,0:T(8,128)(2,1)S(1)} %get-tuple-element.219, bf16[1024,128]{1,0:T(8,128)(2,1)S(1)} %get-tuple-element.220, bf16[1024,128]{1,0:T(8,128)(2,1)S(1)} %get-tuple-element.221, ...), kind=kOutput, calls=%fused_computation.95.clone.1 | convolution fusion | flops 826539008 | bytes 13645824 | tf_op jit(solution)/shard_map/while/body/eval_jaxpr/dot_general | solution.py:37
  164.3 1.9 fusion.60
  166.1 2.0 fusion.61
  174.7 4.1 %fusion.59 = (f32[1024]{0:T(1024)S(1)}, f32[1024,3072]{1,0:T(8,128)S(1)}) fusion(bf16[1024,128]{1,0:T(8,128)(2,1)S(1)} %reshape.574, bf16[1024,128]{1,0:T(8,128)(2,1)S(1)} %get-tuple-element.219, bf16[1024,128]{1,0:T(8,128)(2,1)S(1)} %get-tuple-element.220, bf16[1024,128]{1,0:T(8,128)(2,1)S(1)} %get-tuple-element.221, ...), kind=kOutput, calls=%fused_computation.95.clone.1 | convolution fusion | flops 826539008 | bytes 13645824 | tf_op jit(solution)/shard_map/while/body/eval_jaxpr/dot_general | solution.py:37
  178.8 1.9 fusion.60
  180.7 2.0 fusion.61
  189.3 4.1 %fusion.59 = (f32[1024]{0:T(1024)S(1)}, f32[1024,3072]{1,0:T(8,128)S(1)}) fusion(bf16[1024,128]{1,0:T(8,128)(2,1)S(1)} %reshape.574, bf16[1024,128]{1,0:T(8,128)(2,1)S(1)} %get-tuple-element.219, bf16[1024,128]{1,0:T(8,128)(2,1)S(1)} %get-tuple-element.220, bf16[1024,128]{1,0:T(8,128)(2,1)S(1)} %get-tuple-element.221, ...), kind=kOutput, calls=%fused_computation.95.clone.1 | convolution fusion | flops 826539008 | bytes 13645824 | tf_op jit(solution)/shard_map/while/body/eval_jaxpr/dot_general | solution.py:37
  193.4 1.9 fusion.60
  195.3 2.0 fusion.61
  203.9 4.1 %fusion.59 = (f32[1024]{0:T(1024)S(1)}, f32[1024,3072]{1,0:T(8,128)S(1)}) fusion(bf16[1024,128]{1,0:T(8,128)(2,1)S(1)} %reshape.574, bf16[1024,128]{1,0:T(8,128)(2,1)S(1)} %get-tuple-element.219, bf16[1024,128]{1,0:T(8,128)(2,1)S(1)} %get-tuple-element.220, bf16[1024,128]{1,0:T(8,128)(2,1)S(1)} %get-tuple-element.221, ...), kind=kOutput, calls=%fused_computation.95.clone.1 | convolution fusion | flops 826539008 | bytes 13645824 | tf_op jit(solution)/shard_map/while/body/eval_jaxpr/dot_general | solution.py:37
  208.0 1.9 fusion.60
  209.8 2.0 fusion.61
  218.4 4.1 %fusion.59 = (f32[1024]{0:T(1024)S(1)}, f32[1024,3072]{1,0:T(8,128)S(1)}) fusion(bf16[1024,128]{1,0:T(8,128)(2,1)S(1)} %reshape.574, bf16[1024,128]{1,0:T(8,128)(2,1)S(1)} %get-tuple-element.219, bf16[1024,128]{1,0:T(8,128)(2,1)S(1)} %get-tuple-element.220, bf16[1024,128]{1,0:T(8,128)(2,1)S(1)} %get-tuple-element.221, ...), kind=kOutput, calls=%fused_computation.95.clone.1 | convolution fusion | flops 826539008 | bytes 13645824 | tf_op jit(solution)/shard_map/while/body/eval_jaxpr/dot_general | solution.py:37
  222.5 1.9 fusion.60
  224.4 2.0 fusion.61
  233.0 4.1 %fusion.59 = (f32[1024]{0:T(1024)S(1)}, f32[1024,3072]{1,0:T(8,128)S(1)}) fusion(bf16[1024,128]{1,0:T(8,128)(2,1)S(1)} %reshape.574, bf16[1024,128]{1,0:T(8,128)(2,1)S(1)} %get-tuple-element.219, bf16[1024,128]{1,0:T(8,128)(2,1)S(1)} %get-tuple-element.220, bf16[1024,128]{1,0:T(8,128)(2,1)S(1)} %get-tuple-element.221, ...), kind=kOutput, calls=%fused_computation.95.clone.1 | convolution fusion | flops 826539008 | bytes 13645824 | tf_op jit(solution)/shard_map/while/body/eval_jaxpr/dot_general | solution.py:37
  237.1 1.9 fusion.60
  239.0 2.0 fusion.61
  (149 shorter events, 69.5 us)
Async XLA Ops:
  6.5 3.4 %copy-start.1 = (s32[8,2]{0,1:T(2,128)S(1)}, s32[8,2]{0,1:T(2,128)}, u32[]{:S(2)}) copy-start(s32[8,2]{0,1:T(2,128)} %param.9) | copy-start | bytes 196
  6.5 61.6 %all-gather.3.cloned.1.call-start = ((), (), s32[]{:S(2)}) async-start(), calls=%async_computation.1 | async-start | bytes 5242880 | tf_op jit(solution)/shard_map/all_gather | solution.py:94
  8.9 1.0 copy-start
  11.1 8.8 %collective-permute-start = (s32[1,1]{1,0:T(1,128)}, s32[1,1]{1,0:T(1,128)}, u32[]{:S(2)}, u32[]{:S(2)}) collective-permute-start(s32[1,1]{1,0:T(1,128)} %bitcast.9), channel_id=1, source_target_pairs={{0,4},{4,0},{8,12},{12,8},{16,20},{20,16},{24,28},{28,24},{1,5},{5... | collective-permute-start | bytes 20 | tf_op jit(solution)/shard_map/ppermute | solution.py:78
  14.1 9.5 %collective-permute-start.1 = (s32[1,1]{1,0:T(1,128)}, s32[1,1]{1,0:T(1,128)}, u32[]{:S(2)}, u32[]{:S(2)}) collective-permute-start(s32[1,1]{1,0:T(1,128)} %bitcast.11), channel_id=1, source_target_pairs={{0,8},{4,12},{8,0},{12,4},{16,24},{20,28},{24,16},{28,20},{1,9},{5... | collective-permute-start | bytes 20 | tf_op jit(solution)/shard_map/ppermute | solution.py:78
  15.7 8.0 %collective-permute-start.2 = (s32[1,1]{1,0:T(1,128)}, s32[1,1]{1,0:T(1,128)}, u32[]{:S(2)}, u32[]{:S(2)}) collective-permute-start(s32[1,1]{1,0:T(1,128)} %bitcast.13), channel_id=1, source_target_pairs={{0,12},{4,8},{8,4},{12,0},{16,28},{20,24},{24,20},{28,16},{1,13},{... | collective-permute-start | bytes 20 | tf_op jit(solution)/shard_map/ppermute | solution.py:78
  15.7 8.0 %collective-permute-start.3 = (s32[1,1]{1,0:T(1,128)}, s32[1,1]{1,0:T(1,128)}, u32[]{:S(2)}, u32[]{:S(2)}) collective-permute-start(s32[1,1]{1,0:T(1,128)} %bitcast.15), channel_id=1, source_target_pairs={{0,16},{4,20},{8,24},{12,28},{16,0},{20,4},{24,8},{28,12},{1,17},{... | collective-permute-start | bytes 20 | tf_op jit(solution)/shard_map/ppermute | solution.py:78
  18.7 5.7 %collective-permute-start.4 = (s32[1,1]{1,0:T(1,128)}, s32[1,1]{1,0:T(1,128)}, u32[]{:S(2)}, u32[]{:S(2)}) collective-permute-start(s32[1,1]{1,0:T(1,128)} %bitcast.17), channel_id=1, source_target_pairs={{0,20},{4,16},{8,28},{12,24},{16,4},{20,0},{24,12},{28,8},{1,21},{... | collective-permute-start | bytes 20 | tf_op jit(solution)/shard_map/ppermute | solution.py:78
  20.0 5.6 %collective-permute-start.5 = (s32[1,1]{1,0:T(1,128)}, s32[1,1]{1,0:T(1,128)}, u32[]{:S(2)}, u32[]{:S(2)}) collective-permute-start(s32[1,1]{1,0:T(1,128)} %bitcast.19), channel_id=1, source_target_pairs={{0,24},{4,28},{8,16},{12,20},{16,8},{20,12},{24,0},{28,4},{1,25},{... | collective-permute-start | bytes 20 | tf_op jit(solution)/shard_map/ppermute | solution.py:78
  23.6 6.5 %collective-permute-start.6 = (s32[1,1]{1,0:T(1,128)}, s32[1,1]{1,0:T(1,128)}, u32[]{:S(2)}, u32[]{:S(2)}) collective-permute-start(s32[1,1]{1,0:T(1,128)} %bitcast.21), channel_id=1, source_target_pairs={{0,28},{4,24},{8,20},{12,16},{16,12},{20,8},{24,4},{28,0},{1,29},{... | collective-permute-start | bytes 20 | tf_op jit(solution)/shard_map/ppermute | solution.py:78
  39.0 26.7 %all-to-all-start = ((bf16[8,1,256,256]{3,2,1,0:T(8,128)(2,1)}), bf16[8,1,256,256]{3,2,1,0:T(8,128)(2,1)S(1)}, u32[]{:S(2)}, u32[]{:S(2)}) async-start(bf16[8,1,256,256]{3,2,1,0:T(8,128)(2,1)} %bitcast_select_fusion), calls=%async_computation | async-start | bytes 2097152 | tf_op jit(solution)/shard_map/all_to_all | solution.py:88
  42.6 82.8 %all-gather.5.cloned.1.call-start = ((), (), s32[]{:S(2)}) async-start(), calls=%async_computation.2 | async-start | bytes 10485760 | tf_op jit(solution)/shard_map/all_gather | solution.py:93
Sparse Core Ops, SparseCore 0:
  10.0 37.1 all-gather.2
  68.2 57.1 all-gather.4
